TPU v7x, 256 devices: a whole 4x4x8 slice. The times are simulated.
256 devices in a mesh: gx: 8 (over z), gy: 32 (over y, x, core).
Axes of the slice: x: 4, y: 4, z: 8, core: 2. Of those that a mesh axis runs over, the one named last changes fastest.
Arguments:
- coupling: bfloat16 [8, 256, 1024, 512], P('gx', 'gy'), may hold values from -0.44921875 to 0.44921875
- local_block: bfloat16 [8, 256, 512, 512], P('gx', 'gy'), as said below
- counts: int32 [8, 256], P('gx', 'gy'), may hold values from 1 to 4, as said below
- primal: int32 [8, 256, 512], P('gx', 'gy'), may hold values from 0 to 511
- partner: int32 [3, 8], replicated, may hold values from 0 to 7, as said below
Outputs:
- coarse: float32 [8, 512, 512], P('gx')
Inputs may be any that keep to these rules, and one draw needn't show every extreme that they name: Each row of partner is a perfect matching of the 8 columns: partner[r, partner[r, c]] == c and partner[r, c] != c. `counts`: in each subdomain column at least one subdomain has all 4 blocks live. `primal`: any constraint may hold any number of rows. `local_block`: diagonal entries are positive.
All inputs are finite; a program needn't handle non-finite values. Where the computation divides by a largest or mean magnitude, that divisor is 1e-20 or more.
Results may differ from a plain program's by a relative error of at most 0.00078.
Values sent between devices are 32-bit elements; how exact they have to be, the bound alone decides.
A program may use at most 192 MiB of HBM per device.

v0:
```python
import jax
import jax.numpy as jnp
from jax import lax
from jax.sharding import PartitionSpec as P

BLK = 128
NC = 512
ROUNDS = 3
R = 512


def per_device(coupling, local_block, counts, primal, partner):
    column = lax.axis_index("gx")
    stiff = jnp.diagonal(local_block[0], axis1=1, axis2=2).astype(jnp.float32)
    total = stiff
    for r in range(ROUNDS):
        mate = partner[r, column]
        piece = jax.tree.map(
            lambda part: lax.all_gather(part, "gx", axis=0, tiled=True), stiff[None]
        )
        index = jnp.arange(piece.shape[0], dtype=jnp.int32)
        hit = (index == mate)[:, None, None]
        total = total + (
            jnp.zeros_like(stiff)
            + jnp.sum(jnp.where(hit, piece, jnp.zeros((), jnp.float32)), axis=0)
        )
    weight = stiff / total
    rows = jnp.arange(R, dtype=jnp.int32)
    live = (rows[None, :] < counts[0][:, None] * BLK).astype(jnp.float32)
    gram = jnp.einsum("snr,snq->srq", coupling[0], coupling[0], preferred_element_type=jnp.float32)
    schur = (
        (local_block[0].astype(jnp.float32) - gram) * live[:, :, None] * live[:, None, :]
    ).astype(jnp.bfloat16)
    onehot = primal[0][:, :, None] == jnp.arange(NC, dtype=jnp.int32)[None, None, :]
    basis = jnp.where(onehot, weight[:, :, None], jnp.zeros((), jnp.float32)).astype(jnp.bfloat16)
    image = jnp.einsum("srq,sqk->srk", schur, basis, preferred_element_type=jnp.float32).astype(
        jnp.bfloat16
    )
    tile = jnp.einsum("srk,srl->kl", basis, image, preferred_element_type=jnp.float32)
    summed = lax.psum(tile, "gy")
    scale = 1.0 / jnp.sqrt(jnp.mean(jnp.abs(summed), axis=1) + 1e-06)
    result = summed * scale[:, None] * scale[None, :]
    return result[None]


def solution(mesh):
    placed = (
        P("gx", "gy", None, None),
        P("gx", "gy", None, None),
        P("gx", "gy"),
        P("gx", "gy", None),
        P(),
    )
    return jax.shard_map(
        per_device, mesh=mesh, in_specs=placed, out_specs=P("gx", None, None), check_vma=False
    )
```

profile of v0, /device:TPU:1, one launch (start us, length us, event | category | flops | bytes accessed | tf_op | source)
XLA Modules:
  0.0 238.6 jit_solution(16034111459191862440)
XLA Ops:
  6.5 0.0 all-reduce.2.cloned.1.call-start
  6.5 1.5 constant_dynamic-slice_fusion
  8.0 0.7 iota_compare_fusion.4
  8.7 44.1 %copy.19 = bf16[8,512,512]{0,2,1:T(8,128)(2,1)} copy(bf16[8,512,512]{2,1,0:T(8,128)(2,1)} %bitcast.35) | data formatting | bytes 8388608 | tf_op jit(solution)/shard_map/squeeze | solution.py:14
  52.8 6.5 %gather_fusion = bf16[512,8]{1,0:T(8,128)(2,1)S(1)} fusion(bf16[8,512,512]{0,2,1:T(8,128)(2,1)} %copy.19, s32[512]{0:T(512)S(1)} %bitcast.34), kind=kCustom, calls=%fused_computation | custom fusion | bytes 20480 | tf_op jit(solution)/shard_map/jit(diagonal)/gather | solution.py:14
  59.3 0.1 copy.20
  59.3 23.0 %all-gather = f32[64,512]{1,0:T(8,128)S(1)} all-gather(f32[8,512]{1,0:T(8,128)S(1)} %convert_bitcast_fusion), channel_id=2, replica_groups=mesh['gx'=8,'gy'=32] {'gx'}, dimensions={0}, use_global_device_ids=true | all-gather | bytes 147456 | tf_op jit(solution)/shard_map/all_gather | solution.py:19
  82.4 0.0 copy-start.1
  82.4 0.0 copy-start
  82.4 13.6 %fusion = f32[8,512,512]{2,1,0:T(8,128)} fusion(bf16[1,8,1024,512]{3,2,1,0:T(8,128)(2,1)} %param.5), kind=kOutput, calls=%fused_computation.1 | convolution fusion | flops 4294967296 | bytes 16777216 | tf_op jit(solution)/shard_map/snr,snq->srq/dot_general | solution.py:30
  95.9 0.0 copy-done.1
  95.9 0.1 fusion.21
  96.0 1.2 iota_compare_fusion.2
  97.2 0.1 fusion.18
  97.4 0.0 copy-done
  97.4 10.2 %fusion.15 = f32[512,512]{1,0:T(8,128)} fusion(f32[8,512,512]{2,1,0:T(8,128)} %fusion, f32[8,512]{1,0:T(8,128)S(1)} %fusion.21, bf16[8,512]{1,0:T(8,128)(2,1)S(1)} %add_divide_fusion, s32[8,512]{1,0:T(8,128)S(1)} %bitcast.36, bf16[1,8,512,512]{3,2,1,0:T(8,128)(2,1)} %param.6), kind=kOutput, calls=%fused_computation.14 | convolution fusion | flops 4315938816 | bytes 13672448 | tf_op jit(solution)/shard_map/srk,srl->kl/dot_general | solution.py:39
  107.6 0.0 all-reduce.2.cloned.1.call-update
  107.6 120.4 %all-reduce.2.cloned.1.call-done = f32[512,512]{1,0:T(8,128)} async-done(((f32[512,512]{1,0:T(8,128)}), f32[512,512]{1,0:T(8,128)}) %all-reduce.2.cloned.1.call-update) | async-done | bytes 1048592 | tf_op jit(solution)/shard_map/psum | solution.py:40
  228.0 1.4 abs_reduce_fusion
  229.4 2.4 multiply_bitcast_fusion
  (5 shorter events, 0.0 us)
Async XLA Ops:
  6.5 221.5 %all-reduce.2.cloned.1.call-start = ((), (), s32[]{:S(2)}) async-start(), calls=%async_computation | async-start | bytes 2097152 | tf_op jit(solution)/shard_map/psum | solution.py:40
  82.4 13.6 %copy-start.1 = (s32[1,8]{1,0:T(1,128)S(1)}, s32[1,8]{1,0:T(1,128)}, u32[]{:S(2)}) copy-start(s32[1,8]{1,0:T(1,128)} %param.7) | copy-start | bytes 100
  82.4 15.0 %copy-start = (s32[1,8,512]{2,1,0:T(8,128)S(1)}, s32[1,8,512]{2,1,0:T(8,128)}, u32[]{:S(2)}) copy-start(s32[1,8,512]{2,1,0:T(8,128)} %param.8) | copy-start | bytes 49156
Sparse Core Ops, SparseCore 0:
  107.7 120.2 all-reduce.1
where the time goes:
time: 241 us; the launch traced here: 239 us
  waiting for transfers between devices  120 us (50%)
  local copies, waits for them, and re-layouts  52.1 us (22%)
  matrix products  23.7 us (10%)
  blocking collectives  23 us (10%)
  between operations  13.4 us (6%)
  other arithmetic  5.85 us (2%)
    psum x1, waiting for transfers between devices, per_device(): summed = lax.psum(tile, 'gy')  120 us
    squeeze x1, local copies, waits for them, and re-layouts, per_device(): stiff = jnp.diagonal(local_block[0], axis1=1, axis2=2).astype(jnp.float32)  44.1 us
    all_gather x1, blocking collectives, per_device(): lax.all_gather(part, 'gx', axis=0, tiled=True)  23 us
    dot_general x1, matrix products, per_device(): jnp.einsum('snr,snq->srq', coupling[0], coupling[0], preferred_element_ty...  13.6 us
    dot_general x1, matrix products, per_device(): jnp.einsum('srk,srl->kl', basis, image, preferred_element_type=jnp.float32)  10.2 us
    gather x2, local copies, waits for them, and re-layouts, per_device(): stiff = jnp.diagonal(local_block[0], axis1=1, axis2=2).astype(jnp.float32)  6.53 us
  transfers between devices with their start and end apart: 1, of which 1 were waited for; matrix products, arithmetic and copies ran while one was open for 0% of the time, Pallas kernels for 0%

commit v1 on v0

--- a/solution.py
+++ b/solution.py
@@ -37,7 +37,9 @@
         jnp.bfloat16
     )
     tile = jnp.einsum("srk,srl->kl", basis, image, preferred_element_type=jnp.float32)
-    summed = lax.psum(tile, "gy")
+    summed = tile
+    for hop in (1, 2, 4, 8, 16):
+        summed = summed + lax.ppermute(summed, "gy", [(dev, dev ^ hop) for dev in range(32)])
     scale = 1.0 / jnp.sqrt(jnp.mean(jnp.abs(summed), axis=1) + 1e-06)
     result = summed * scale[:, None] * scale[None, :]
     return result[None]

time: 241 us -> 213 us (0.88)
  the two profiles are of different devices: /device:TPU:1 before, /device:TPU:6 now
where the time goes in v1:
time: 213 us; the launch traced here: 210 us
  waiting for transfers between devices  94.8 us (45%)
  local copies, waits for them, and re-layouts  53.6 us (25%)
  blocking collectives  28.3 us (13%)
  matrix products  22.5 us (11%)
  starting transfers between devices  7.62 us (4%)
  other arithmetic  3.33 us (2%)
    ppermute x5, waiting for transfers between devices, per_device(): lax.ppermute(summed, 'gy', [(dev, dev ^ hop) for dev in range(32)])  94.8 us
    squeeze x1, local copies, waits for them, and re-layouts, per_device(): stiff = jnp.diagonal(local_block[0], axis1=1, axis2=2).astype(jnp.float32)  45.1 us
    all_gather x1, blocking collectives, per_device(): lax.all_gather(part, 'gx', axis=0, tiled=True)  28.3 us
    dot_general x1, matrix products, per_device(): jnp.einsum('snr,snq->srq', coupling[0], coupling[0], preferred_element_ty...  13.5 us
    ppermute x5, starting transfers between devices, per_device(): lax.ppermute(summed, 'gy', [(dev, dev ^ hop) for dev in range(32)])  7.62 us
    gather x2, local copies, waits for them, and re-layouts, per_device(): stiff = jnp.diagonal(local_block[0], axis1=1, axis2=2).astype(jnp.float32)  6.55 us
    dot_general x1, matrix products, per_device(): jnp.einsum('srq,sqk->srk', schur, basis, preferred_element_type=jnp.float32)  6.1 us
  transfers between devices with their start and end apart: 5, of which 5 were waited for; matrix products, arithmetic and copies ran while one was open for 0% of the time, Pallas kernels for 0%

profile of v1, /device:TPU:6, one launch (start us, length us, event | category | flops | bytes accessed | tf_op | source)
XLA Modules:
  0.0 210.2 jit_solution(6395172215831171771)
XLA Ops:
  0.0 0.0 copy-start
  0.0 45.1 %copy.22 = bf16[8,512,512]{0,2,1:T(8,128)(2,1)} copy(bf16[8,512,512]{2,1,0:T(8,128)(2,1)} %bitcast.42) | data formatting | bytes 8388608 | tf_op jit(solution)/shard_map/squeeze | solution.py:14
  45.1 6.5 %gather_fusion = bf16[512,8]{1,0:T(8,128)(2,1)S(1)} fusion(bf16[8,512,512]{0,2,1:T(8,128)(2,1)} %copy.22, s32[512]{0:T(512)S(1)} %bitcast.41), kind=kCustom, calls=%fused_computation | custom fusion | bytes 20480 | tf_op jit(solution)/shard_map/jit(diagonal)/gather | solution.py:14
  51.6 0.1 copy.23
  51.7 28.3 %all-gather = f32[64,512]{1,0:T(8,128)S(1)} all-gather(f32[8,512]{1,0:T(8,128)S(1)} %convert_bitcast_fusion), channel_id=2, replica_groups=mesh['gx'=8,'gy'=32] {'gx'}, dimensions={0}, use_global_device_ids=true | all-gather | bytes 147456 | tf_op jit(solution)/shard_map/all_gather | solution.py:19
  80.0 0.6 constant_dynamic-slice_fusion
  80.6 0.6 iota_compare_fusion.4
  81.1 0.0 copy-start.2
  81.1 0.0 copy-start.1
  81.2 13.5 %fusion = f32[8,512,512]{2,1,0:T(8,128)} fusion(bf16[1,8,1024,512]{3,2,1,0:T(8,128)(2,1)} %param.5), kind=kOutput, calls=%fused_computation.1 | convolution fusion | flops 4294967296 | bytes 16777216 | tf_op jit(solution)/shard_map/snr,snq->srq/dot_general | solution.py:30
  94.7 0.1 fusion.21
  94.8 1.3 iota_compare_fusion.2
  96.1 0.1 fusion.18
  96.2 6.1 %fusion.29 = bf16[8,512,512]{2,1,0:T(8,128)(2,1)S(1)} fusion(f32[8,512,512]{2,1,0:T(8,128)} %fusion, f32[8,512]{1,0:T(8,128)S(1)} %fusion.21, bf16[8,512]{1,0:T(8,128)(2,1)S(1)} %add_divide_fusion, s32[8,512]{1,0:T(8,128)S(1)} %bitcast.43, bf16[1,8,512,512]{3,2,1,0:T(8,128)(2,1)} %param.6), kind=kOutput, calls=%fused_computation.8.clone.clone.clone.2 | convolution fusion | flops 2164260864 | bytes 16818176 | tf_op jit(solution)/shard_map/srq,sqk->srk/dot_general | solution.py:36
  102.3 2.9 %fusion.15 = f32[512,512]{0,1:T(8,128)S(1)} fusion(bf16[8,512]{1,0:T(8,128)(2,1)S(1)} %add_divide_fusion, s32[8,512]{1,0:T(8,128)S(1)} %bitcast.44, bf16[8,512,512]{2,1,0:T(8,128)(2,1)S(1)} %fusion.29), kind=kOutput, calls=%fused_computation.14 | convolution fusion | flops 2151677952 | bytes 5267456 | tf_op jit(solution)/shard_map/srk,srl->kl/dot_general | solution.py:39
  105.2 0.1 collective-permute-start
  105.3 2.6 %collective-permute-done = f32[512,512]{0,1:T(8,128)S(1)} collective-permute-done((f32[512,512]{0,1:T(8,128)S(1)}, f32[512,512]{0,1:T(8,128)S(1)}, u32[]{:S(2)}, u32[]{:S(2)}) %collective-permute-start) | collective-permute-done | bytes 1048608 | tf_op jit(solution)/shard_map/ppermute | solution.py:42
  107.9 0.2 add.63
  108.2 0.9 collective-permute-start.1
  109.1 24.4 %collective-permute-done.1 = f32[512,512]{0,1:T(8,128)S(1)} collective-permute-done((f32[512,512]{0,1:T(8,128)S(1)}, f32[512,512]{0,1:T(8,128)S(1)}, u32[]{:S(2)}, u32[]{:S(2)}) %collective-permute-start.1) | collective-permute-done | bytes 1048608 | tf_op jit(solution)/shard_map/ppermute | solution.py:42
  133.4 0.2 add.64
  133.7 1.7 collective-permute-start.2
  135.3 24.5 %collective-permute-done.2 = f32[512,512]{0,1:T(8,128)S(1)} collective-permute-done((f32[512,512]{0,1:T(8,128)S(1)}, f32[512,512]{0,1:T(8,128)S(1)}, u32[]{:S(2)}, u32[]{:S(2)}) %collective-permute-start.2) | collective-permute-done | bytes 1048608 | tf_op jit(solution)/shard_map/ppermute | solution.py:42
  159.8 0.2 add.65
  160.0 1.7 collective-permute-start.3
  161.7 21.9 %collective-permute-done.3 = f32[512,512]{0,1:T(8,128)S(1)} collective-permute-done((f32[512,512]{0,1:T(8,128)S(1)}, f32[512,512]{0,1:T(8,128)S(1)}, u32[]{:S(2)}, u32[]{:S(2)}) %collective-permute-start.3) | collective-permute-done | bytes 1048608 | tf_op jit(solution)/shard_map/ppermute | solution.py:42
  183.5 0.2 add.66
  183.8 3.3 %collective-permute-start.4 = (f32[512,512]{0,1:T(8,128)S(1)}, f32[512,512]{0,1:T(8,128)S(1)}, u32[]{:S(2)}, u32[]{:S(2)}) collective-permute-start(f32[512,512]{0,1:T(8,128)S(1)} %add.66), channel_id=1, source_target_pairs={{0,16},{1,17},{2,18},{3,19},{4,20},{5,21},{6,22},{7,23},{8,24},{9,... | collective-permute-start | bytes 3145736 | tf_op jit(solution)/shard_map/ppermute | solution.py:42
  187.0 21.4 %collective-permute-done.4 = f32[512,512]{0,1:T(8,128)S(1)} collective-permute-done((f32[512,512]{0,1:T(8,128)S(1)}, f32[512,512]{0,1:T(8,128)S(1)}, u32[]{:S(2)}, u32[]{:S(2)}) %collective-permute-start.4) | collective-permute-done | bytes 1048608 | tf_op jit(solution)/shard_map/ppermute | solution.py:42
  208.5 0.3 abs_reduce_fusion
  208.8 0.2 multiply_bitcast_fusion
  208.9 1.3 copy.26
  (8 shorter events, 0.0 us)
Async XLA Ops:
  0.0 80.0 %copy-start = (s32[3,8]{1,0:T(4,128)S(1)}, s32[3,8]{1,0:T(4,128)}, u32[]{:S(2)}) copy-start(s32[3,8]{1,0:T(4,128)} %param.9) | copy-start | bytes 292
  81.1 13.6 %copy-start.2 = (s32[1,8]{1,0:T(1,128)S(1)}, s32[1,8]{1,0:T(1,128)}, u32[]{:S(2)}) copy-start(s32[1,8]{1,0:T(1,128)} %param.7) | copy-start | bytes 100
  81.1 15.0 %copy-start.1 = (s32[1,8,512]{2,1,0:T(8,128)S(1)}, s32[1,8,512]{2,1,0:T(8,128)}, u32[]{:S(2)}) copy-start(s32[1,8,512]{2,1,0:T(8,128)} %param.8) | copy-start | bytes 49156
  105.2 2.7 %collective-permute-start = (f32[512,512]{0,1:T(8,128)S(1)}, f32[512,512]{0,1:T(8,128)S(1)}, u32[]{:S(2)}, u32[]{:S(2)}) collective-permute-start(f32[512,512]{0,1:T(8,128)S(1)} %fusion.15), channel_id=1, source_target_pairs={{0,1},{1,0},{2,3},{3,2},{4,5},{5,4},{6,7},{7,6},{8,9},{9,8},{10,11... | collective-permute-start | bytes 3145736 | tf_op jit(solution)/shard_map/ppermute | solution.py:42
  108.2 25.3 %collective-permute-start.1 = (f32[512,512]{0,1:T(8,128)S(1)}, f32[512,512]{0,1:T(8,128)S(1)}, u32[]{:S(2)}, u32[]{:S(2)}) collective-permute-start(f32[512,512]{0,1:T(8,128)S(1)} %add.63), channel_id=1, source_target_pairs={{0,2},{1,3},{2,0},{3,1},{4,6},{5,7},{6,4},{7,5},{8,10},{9,11},{10,... | collective-permute-start | bytes 3145736 | tf_op jit(solution)/shard_map/ppermute | solution.py:42
  133.7 26.1 %collective-permute-start.2 = (f32[512,512]{0,1:T(8,128)S(1)}, f32[512,512]{0,1:T(8,128)S(1)}, u32[]{:S(2)}, u32[]{:S(2)}) collective-permute-start(f32[512,512]{0,1:T(8,128)S(1)} %add.64), channel_id=1, source_target_pairs={{0,4},{1,5},{2,6},{3,7},{4,0},{5,1},{6,2},{7,3},{8,12},{9,13},{10,... | collective-permute-start | bytes 3145736 | tf_op jit(solution)/shard_map/ppermute | solution.py:42
  160.0 23.5 %collective-permute-start.3 = (f32[512,512]{0,1:T(8,128)S(1)}, f32[512,512]{0,1:T(8,128)S(1)}, u32[]{:S(2)}, u32[]{:S(2)}) collective-permute-start(f32[512,512]{0,1:T(8,128)S(1)} %add.65), channel_id=1, source_target_pairs={{0,8},{1,9},{2,10},{3,11},{4,12},{5,13},{6,14},{7,15},{8,0},{9,1},... | collective-permute-start | bytes 3145736 | tf_op jit(solution)/shard_map/ppermute | solution.py:42
  183.8 24.7 %collective-permute-start.4 = (f32[512,512]{0,1:T(8,128)S(1)}, f32[512,512]{0,1:T(8,128)S(1)}, u32[]{:S(2)}, u32[]{:S(2)}) collective-permute-start(f32[512,512]{0,1:T(8,128)S(1)} %add.66), channel_id=1, source_target_pairs={{0,16},{1,17},{2,18},{3,19},{4,20},{5,21},{6,22},{7,23},{8,24},{9,... | collective-permute-start | bytes 3145736 | tf_op jit(solution)/shard_map/ppermute | solution.py:42
